TPU v7x, 512 devices: a whole 4x4x16 slice. The times are simulated.
512 devices in a mesh: dom: 128 (over x, z, core), blk: 4 (over y).
Axes of the slice: x: 4, y: 4, z: 16, core: 2. Of those that a mesh axis runs over, the one named last changes fastest.
Arguments:
- degree: int32 [1024], P('dom'), may hold values from 1 to 3
- face_elem: int32 [4096], P('dom'), may hold values from 0 to 7
- face_side: int32 [4096], P('dom'), may hold values from 0 to 8, as said below
- face_peer: int32 [4096], P('dom'), may hold values from 0 to 7
- coupling: bfloat16 [4096, 320, 320], P('dom', 'blk'), may hold values from -0.078125 to 0.078125
- inv_diag: float32 [1024, 320], P('dom', 'blk'), may hold values from 0.5 to 2
- inv_off: bfloat16 [1024, 320, 320], P('dom', 'blk'), may hold values from -0.109375 to 0.109375
- source: float32 [1024, 320], P('dom', 'blk'), may hold values from -6 to 6
- residual: float32 [1024, 320], P('dom', 'blk'), may hold values from -0.6 to 0.6
Outputs:
- adjoint: float32 [1024, 320], P('dom', 'blk')
- indicator: float32 [1024], P('dom')
Inputs may be any that keep to these rules, and one draw needn't show every extreme that they name: `face_side`: among the 32 faces of one partition (aligned blocks of 32 rows) each side from 1 to 8 is named by at least 2 and at most 4 faces, and one side by exactly 4; the remaining faces have side 0.
All inputs are finite; a program needn't handle non-finite values.
Results may differ from a plain program's by a relative error of at most 0.004.
Values may be sent and summed in bfloat16 or wider, within the bound.
No kernel may reach another device: no remote copies, remote signals or barrier semaphores. Data moves between devices by JAX's collectives and lax.ppermute only.
A program may use at most 64 MiB of HBM per device.

v0:
```python
import jax
import jax.numpy as jnp
from jax import lax
from jax.sharding import PartitionSpec as P

MODES = 64
SWEEPS = 2
NEIGH = 8


def from_behind(block, axis, distance):
    devices = range(lax.axis_size(axis))
    route = [((i - distance) % len(devices), i) for i in devices]
    return lax.ppermute(block, axis, route)


def full_rows(values):
    return lax.all_gather(values, "blk", axis=1, tiled=True)


def local(degree, face_elem, face_side, face_peer, coupling, inv_diag, inv_off, source, residual):
    width = coupling.shape[2]
    quarter = source.shape[1]
    elements = source.shape[0]
    faces = coupling.shape[0]
    neigh = NEIGH
    half_count = neigh // 2
    capacity = faces // neigh
    offsets = [step_size for step_size in range(1, half_count + 1)] + [
        -step_size for step_size in range(1, half_count + 1)
    ]
    first_row = lax.axis_index("blk") * quarter
    limit = (degree + 1) ** 3 * MODES // 64
    modes = jnp.arange(width, dtype=jnp.int32) % MODES
    mask_full = (modes[None, :] < limit[:, None]).astype(jnp.float32)
    mask_rows = lax.dynamic_slice_in_dim(mask_full, first_row, quarter, 1)
    codes = jnp.arange(neigh + 1, dtype=jnp.int32)
    onehot = (face_side[:, None] == codes[None, :]).astype(jnp.int32)
    before = jnp.cumsum(onehot, axis=0) - onehot
    slot_index = jnp.sum(before * onehot, axis=1)
    crossing = face_side > 0
    inner = jnp.where(crossing, 0.0, 1.0).astype(jnp.float32)
    position = jnp.where(crossing, (face_side - 1) * capacity + slot_index, neigh * capacity)
    safe_position = jnp.minimum(position, neigh * capacity - 1)
    wanted = (
        jnp.zeros((neigh * capacity,), jnp.int32)
        .at[position]
        .set(face_peer, mode="drop")
        .reshape(neigh, capacity)
    )
    requested = jnp.stack(
        [from_behind(wanted[side_num], "dom", offsets[side_num]) for side_num in range(neigh)]
    )
    requested_flat = requested.reshape(-1)

    def invert(values_full):
        own_part = lax.dynamic_slice_in_dim(values_full, first_row, quarter, 1)
        product = jnp.einsum("eij,ej->ei", inv_off, values_full, preferred_element_type=jnp.float32)
        return inv_diag * own_part.astype(jnp.float32) + product

    source_half = (source * mask_rows).astype(jnp.bfloat16)
    base_state = invert(full_rows(source_half)) * mask_rows
    adjoint = base_state
    for sweep_index in range(SWEEPS):
        state_rows = adjoint.astype(jnp.bfloat16)
        state_full = full_rows(state_rows)
        outgoing = state_full[requested]
        incoming = jnp.stack(
            [
                from_behind(outgoing[side_num], "dom", -offsets[side_num])
                for side_num in range(neigh)
            ]
        ).reshape(-1, width)
        peer_state = jnp.where(crossing[:, None], incoming[safe_position], state_full[face_peer])
        elem_state = state_rows[face_elem]
        local_terms = jnp.einsum(
            "fij,fj->fi", coupling, peer_state, preferred_element_type=jnp.float32
        )
        transposed = jnp.einsum(
            "fij,fi->fj", coupling, elem_state, preferred_element_type=jnp.float32
        )
        own_terms = jnp.zeros((elements, quarter), jnp.float32).at[face_elem].add(local_terms)
        partial_value = (
            jnp.zeros((elements, width), jnp.float32).at[face_peer].add(transposed * inner[:, None])
        )
        outbound = (
            jnp.zeros((neigh * capacity, width), jnp.float32)
            .at[position]
            .set(transposed, mode="drop")
            .reshape(neigh, capacity, width)
        )
        returned = jnp.stack(
            [from_behind(outbound[side_num], "dom", offsets[side_num]) for side_num in range(neigh)]
        ).reshape(-1, width)
        partial_value = partial_value.at[requested_flat].add(returned)
        middle = lax.dynamic_slice_in_dim(partial_value, first_row, quarter, 1) + own_terms
        partial_value = lax.dynamic_update_slice_in_dim(partial_value, middle, first_row, 1)
        summed = lax.psum(partial_value, "blk")
        coupled_half = (summed * mask_full).astype(jnp.bfloat16)
        adjoint = (base_state - invert(coupled_half)) * mask_rows
    weights = jnp.sum(adjoint * residual * mask_rows, axis=1)
    indicator = lax.psum(weights, "blk")
    return (adjoint, indicator)


def solution(mesh):
    in_specs = (
        P("dom"),
        P("dom"),
        P("dom"),
        P("dom"),
        P("dom", "blk", None),
        P("dom", "blk"),
        P("dom", "blk", None),
        P("dom", "blk"),
        P("dom", "blk"),
    )
    out_specs = (P("dom", "blk"), P("dom"))
    return jax.shard_map(local, mesh=mesh, in_specs=in_specs, out_specs=out_specs, check_vma=False)
```

profile of v0, /device:TPU:64, one launch (start us, length us, event | category | flops | bytes accessed | tf_op | source)
XLA Modules:
  0.0 313.2 jit_solution(9358824529545259234)
XLA Ops:
  5.9 3.8 %collective-permute-start.1 = (s32[4]{0:T(128)S(1)}, s32[4]{0:T(128)S(1)}, u32[]{:S(2)}, u32[]{:S(2)}) collective-permute-start(s32[4]{0:T(128)S(1)} %get-tuple-element.44), channel_id=1, source_target_pairs={{504,0},{508,4},{0,8},{4,12},{8,16},{12,20},{16,24},{20,28},{24,32... | collective-permute-start | bytes 56 | tf_op jit(solution)/shard_map/ppermute | solution.py:14
  9.7 6.4 %collective-permute-start.2 = (s32[4]{0:T(128)S(1)}, s32[4]{0:T(128)S(1)}, u32[]{:S(2)}, u32[]{:S(2)}) collective-permute-start(s32[4]{0:T(128)S(1)} %get-tuple-element.43), channel_id=1, source_target_pairs={{500,0},{504,4},{508,8},{0,12},{4,16},{8,20},{12,24},{16,28},{20,3... | collective-permute-start | bytes 56 | tf_op jit(solution)/shard_map/ppermute | solution.py:14
  16.1 5.2 %collective-permute-start.3 = (s32[4]{0:T(128)S(1)}, s32[4]{0:T(128)S(1)}, u32[]{:S(2)}, u32[]{:S(2)}) collective-permute-start(s32[4]{0:T(128)S(1)} %get-tuple-element.42), channel_id=1, source_target_pairs={{496,0},{500,4},{504,8},{508,12},{0,16},{4,20},{8,24},{12,28},{16,... | collective-permute-start | bytes 56 | tf_op jit(solution)/shard_map/ppermute | solution.py:14
  26.7 11.3 %all-gather = bf16[4,80,8]{1,2,0:T(8,128)(2,1)S(1)} all-gather(bf16[1,80,8]{1,2,0:T(8,128)(2,1)S(1)} %fusion.36), channel_id=1, replica_groups=mesh['dom'=128,'blk'=4] {'blk'}, dimensions={0}, use_global_device_ids=true | all-gather | bytes 6400 | tf_op jit(solution)/shard_map/all_gather | solution.py:18
  43.5 10.4 %all-gather.1 = bf16[4,80,8]{1,2,0:T(8,128)(2,1)S(1)} all-gather(bf16[1,80,8]{1,2,0:T(8,128)(2,1)S(1)} %bitcast.165), channel_id=1, replica_groups=mesh['dom'=128,'blk'=4] {'blk'}, dimensions={0}, use_global_device_ids=true | all-gather | bytes 6400 | tf_op jit(solution)/shard_map/all_gather | solution.py:18
  58.7 5.2 %collective-permute-start.7 = (s32[4]{0:T(128)S(1)}, s32[4]{0:T(128)S(1)}, u32[]{:S(2)}, u32[]{:S(2)}) collective-permute-start(s32[4]{0:T(128)S(1)} %get-tuple-element.38), channel_id=1, source_target_pairs={{16,0},{20,4},{24,8},{28,12},{32,16},{36,20},{40,24},{44,28},{48,3... | collective-permute-start | bytes 56 | tf_op jit(solution)/shard_map/ppermute | solution.py:14
  63.9 3.5 %collective-permute-start.8 = (f32[4,320]{1,0:T(4,128)S(1)}, f32[4,320]{1,0:T(4,128)S(1)}, u32[]{:S(2)}, u32[]{:S(2)}) collective-permute-start(f32[4,320]{1,0:T(4,128)S(1)} %get-tuple-element.21), channel_id=1, source_target_pairs={{508,0},{0,4},{4,8},{8,12},{12,16},{16,20},{20,24},{24,28},{28,32}... | collective-permute-start | bytes 15368 | tf_op jit(solution)/shard_map/ppermute | solution.py:14
  69.6 3.9 %collective-permute-start.10 = (f32[4,320]{1,0:T(4,128)S(1)}, f32[4,320]{1,0:T(4,128)S(1)}, u32[]{:S(2)}, u32[]{:S(2)}) collective-permute-start(f32[4,320]{1,0:T(4,128)S(1)} %get-tuple-element.19), channel_id=1, source_target_pairs={{500,0},{504,4},{508,8},{0,12},{4,16},{8,20},{12,24},{16,28},{20,3... | collective-permute-start | bytes 15368 | tf_op jit(solution)/shard_map/ppermute | solution.py:14
  73.6 4.8 %collective-permute-start.11 = (f32[4,320]{1,0:T(4,128)S(1)}, f32[4,320]{1,0:T(4,128)S(1)}, u32[]{:S(2)}, u32[]{:S(2)}) collective-permute-start(f32[4,320]{1,0:T(4,128)S(1)} %get-tuple-element.18), channel_id=1, source_target_pairs={{496,0},{500,4},{504,8},{508,12},{0,16},{4,20},{8,24},{12,28},{16,... | collective-permute-start | bytes 15368 | tf_op jit(solution)/shard_map/ppermute | solution.py:14
  88.4 8.1 %collective-permute-start.18 = (bf16[4,320]{1,0:T(4,128)(2,1)S(1)}, bf16[4,320]{1,0:T(4,128)(2,1)S(1)}, u32[]{:S(2)}, u32[]{:S(2)}) collective-permute-start(bf16[4,320]{1,0:T(4,128)(2,1)S(1)} %get-tuple-element.35), channel_id=1, source_target_pairs={{12,0},{16,4},{20,8},{24,12},{28,16},{32,20},{36,24},{40,28},{44,3... | collective-permute-start | bytes 7688 | tf_op jit(solution)/shard_map/ppermute | solution.py:14
  97.8 3.6 %collective-permute-start.19 = (bf16[4,320]{1,0:T(4,128)(2,1)S(1)}, bf16[4,320]{1,0:T(4,128)(2,1)S(1)}, u32[]{:S(2)}, u32[]{:S(2)}) collective-permute-start(bf16[4,320]{1,0:T(4,128)(2,1)S(1)} %get-tuple-element.34), channel_id=1, source_target_pairs={{16,0},{20,4},{24,8},{28,12},{32,16},{36,20},{40,24},{44,28},{48,3... | collective-permute-start | bytes 7688 | tf_op jit(solution)/shard_map/ppermute | solution.py:14
  101.5 4.0 %collective-permute-done.19 = bf16[4,320]{1,0:T(4,128)(2,1)S(1)} collective-permute-done((bf16[4,320]{1,0:T(4,128)(2,1)S(1)}, bf16[4,320]{1,0:T(4,128)(2,1)S(1)}, u32[]{:S(2)}, u32[]{:S(2)}) %collective-permute-start.19) | collective-permute-done | bytes 2592 | tf_op jit(solution)/shard_map/ppermute | solution.py:14
  107.4 7.2 %collective-permute-done.20 = bf16[4,320]{1,0:T(4,128)(2,1)S(1)} collective-permute-done((bf16[4,320]{1,0:T(4,128)(2,1)S(1)}, bf16[4,320]{1,0:T(4,128)(2,1)S(1)}, u32[]{:S(2)}, u32[]{:S(2)}) %collective-permute-start.20) | collective-permute-done | bytes 2592 | tf_op jit(solution)/shard_map/ppermute | solution.py:14
  116.5 3.5 %collective-permute-done.21 = bf16[4,320]{1,0:T(4,128)(2,1)S(1)} collective-permute-done((bf16[4,320]{1,0:T(4,128)(2,1)S(1)}, bf16[4,320]{1,0:T(4,128)(2,1)S(1)}, u32[]{:S(2)}, u32[]{:S(2)}) %collective-permute-start.21) | collective-permute-done | bytes 2592 | tf_op jit(solution)/shard_map/ppermute | solution.py:14
  122.0 4.4 %collective-permute-done.22 = bf16[4,320]{1,0:T(4,128)(2,1)S(1)} collective-permute-done((bf16[4,320]{1,0:T(4,128)(2,1)S(1)}, bf16[4,320]{1,0:T(4,128)(2,1)S(1)}, u32[]{:S(2)}, u32[]{:S(2)}) %collective-permute-start.22) | collective-permute-done | bytes 2592 | tf_op jit(solution)/shard_map/ppermute | solution.py:14
  128.6 13.6 %collective-permute-done.23 = bf16[4,320]{1,0:T(4,128)(2,1)S(1)} collective-permute-done((bf16[4,320]{1,0:T(4,128)(2,1)S(1)}, bf16[4,320]{1,0:T(4,128)(2,1)S(1)}, u32[]{:S(2)}, u32[]{:S(2)}) %collective-permute-start.23) | collective-permute-done | bytes 2592 | tf_op jit(solution)/shard_map/ppermute | solution.py:14
  145.6 3.4 %collective-permute-start.13 = (f32[4,320]{1,0:T(4,128)S(1)}, f32[4,320]{1,0:T(4,128)S(1)}, u32[]{:S(2)}, u32[]{:S(2)}) collective-permute-start(f32[4,320]{1,0:T(4,128)S(1)} %get-tuple-element.16), channel_id=1, source_target_pairs={{8,0},{12,4},{16,8},{20,12},{24,16},{28,20},{32,24},{36,28},{40,32... | collective-permute-start | bytes 15368 | tf_op jit(solution)/shard_map/ppermute | solution.py:14
  149.0 6.8 %collective-permute-start.14 = (f32[4,320]{1,0:T(4,128)S(1)}, f32[4,320]{1,0:T(4,128)S(1)}, u32[]{:S(2)}, u32[]{:S(2)}) collective-permute-start(f32[4,320]{1,0:T(4,128)S(1)} %get-tuple-element.15), channel_id=1, source_target_pairs={{12,0},{16,4},{20,8},{24,12},{28,16},{32,20},{36,24},{40,28},{44,3... | collective-permute-start | bytes 15368 | tf_op jit(solution)/shard_map/ppermute | solution.py:14
  157.9 5.6 %collective-permute-done.15 = f32[4,320]{1,0:T(4,128)S(1)} collective-permute-done((f32[4,320]{1,0:T(4,128)S(1)}, f32[4,320]{1,0:T(4,128)S(1)}, u32[]{:S(2)}, u32[]{:S(2)}) %collective-permute-start.15) | collective-permute-done | bytes 5152 | tf_op jit(solution)/shard_map/ppermute | solution.py:14
  165.4 15.8 %psum.21 = bf16[8,320]{1,0:T(8,128)(2,1)S(1)} all-reduce(f32[8,320]{1,0:T(8,128)S(1)} %dynamic_update_slice.6), channel_id=1, replica_groups=mesh['dom'=128,'blk'=4] {'blk'}, use_global_device_ids=true, to_apply=%region_7.8 | all-reduce | flops 2560 | bytes 15360 | tf_op jit(solution)/shard_map/psum | solution.py:98
  183.4 10.4 %all-gather.2 = bf16[4,80,8]{1,2,0:T(8,128)(2,1)S(1)} all-gather(bf16[1,80,8]{1,2,0:T(8,128)(2,1)S(1)} %bitcast.166), channel_id=1, replica_groups=mesh['dom'=128,'blk'=4] {'blk'}, dimensions={0}, use_global_device_ids=true | all-gather | bytes 6400 | tf_op jit(solution)/shard_map/all_gather | solution.py:18
  200.5 3.6 %collective-permute-start.25 = (f32[4,320]{1,0:T(4,128)S(1)}, f32[4,320]{1,0:T(4,128)S(1)}, u32[]{:S(2)}, u32[]{:S(2)}) collective-permute-start(f32[4,320]{1,0:T(4,128)S(1)} %get-tuple-element.12), channel_id=1, source_target_pairs={{504,0},{508,4},{0,8},{4,12},{8,16},{12,20},{16,24},{20,28},{24,32... | collective-permute-start | bytes 15368 | tf_op jit(solution)/shard_map/ppermute | solution.py:14
  213.5 5.9 %collective-permute-start.34 = (bf16[4,320]{1,0:T(4,128)(2,1)S(1)}, bf16[4,320]{1,0:T(4,128)(2,1)S(1)}, u32[]{:S(2)}, u32[]{:S(2)}) collective-permute-start(bf16[4,320]{1,0:T(4,128)(2,1)S(1)} %get-tuple-element.27), channel_id=1, source_target_pairs={{12,0},{16,4},{20,8},{24,12},{28,16},{32,20},{36,24},{40,28},{44,3... | collective-permute-start | bytes 7688 | tf_op jit(solution)/shard_map/ppermute | solution.py:14
  220.7 5.3 %collective-permute-start.35 = (bf16[4,320]{1,0:T(4,128)(2,1)S(1)}, bf16[4,320]{1,0:T(4,128)(2,1)S(1)}, u32[]{:S(2)}, u32[]{:S(2)}) collective-permute-start(bf16[4,320]{1,0:T(4,128)(2,1)S(1)} %get-tuple-element.26), channel_id=1, source_target_pairs={{16,0},{20,4},{24,8},{28,12},{32,16},{36,20},{40,24},{44,28},{48,3... | collective-permute-start | bytes 7688 | tf_op jit(solution)/shard_map/ppermute | solution.py:14
  231.4 6.0 %collective-permute-done.36 = bf16[4,320]{1,0:T(4,128)(2,1)S(1)} collective-permute-done((bf16[4,320]{1,0:T(4,128)(2,1)S(1)}, bf16[4,320]{1,0:T(4,128)(2,1)S(1)}, u32[]{:S(2)}, u32[]{:S(2)}) %collective-permute-start.36) | collective-permute-done | bytes 2592 | tf_op jit(solution)/shard_map/ppermute | solution.py:14
  239.3 4.8 %collective-permute-done.37 = bf16[4,320]{1,0:T(4,128)(2,1)S(1)} collective-permute-done((bf16[4,320]{1,0:T(4,128)(2,1)S(1)}, bf16[4,320]{1,0:T(4,128)(2,1)S(1)}, u32[]{:S(2)}, u32[]{:S(2)}) %collective-permute-start.37) | collective-permute-done | bytes 2592 | tf_op jit(solution)/shard_map/ppermute | solution.py:14
  246.1 4.6 %collective-permute-done.38 = bf16[4,320]{1,0:T(4,128)(2,1)S(1)} collective-permute-done((bf16[4,320]{1,0:T(4,128)(2,1)S(1)}, bf16[4,320]{1,0:T(4,128)(2,1)S(1)}, u32[]{:S(2)}, u32[]{:S(2)}) %collective-permute-start.38) | collective-permute-done | bytes 2592 | tf_op jit(solution)/shard_map/ppermute | solution.py:14
  252.7 12.3 %collective-permute-done.39 = bf16[4,320]{1,0:T(4,128)(2,1)S(1)} collective-permute-done((bf16[4,320]{1,0:T(4,128)(2,1)S(1)}, bf16[4,320]{1,0:T(4,128)(2,1)S(1)}, u32[]{:S(2)}, u32[]{:S(2)}) %collective-permute-start.39) | collective-permute-done | bytes 2592 | tf_op jit(solution)/shard_map/ppermute | solution.py:14
  271.9 6.8 %collective-permute-start.30 = (f32[4,320]{1,0:T(4,128)S(1)}, f32[4,320]{1,0:T(4,128)S(1)}, u32[]{:S(2)}, u32[]{:S(2)}) collective-permute-start(f32[4,320]{1,0:T(4,128)S(1)} %get-tuple-element.7), channel_id=1, source_target_pairs={{12,0},{16,4},{20,8},{24,12},{28,16},{32,20},{36,24},{40,28},{44,3... | collective-permute-start | bytes 15368 | tf_op jit(solution)/shard_map/ppermute | solution.py:14
  280.7 5.6 %collective-permute-done.31 = f32[4,320]{1,0:T(4,128)S(1)} collective-permute-done((f32[4,320]{1,0:T(4,128)S(1)}, f32[4,320]{1,0:T(4,128)S(1)}, u32[]{:S(2)}, u32[]{:S(2)}) %collective-permute-start.31) | collective-permute-done | bytes 5152 | tf_op jit(solution)/shard_map/ppermute | solution.py:14
  288.2 14.3 %psum.22 = bf16[8,320]{1,0:T(8,128)(2,1)S(1)} all-reduce(f32[8,320]{1,0:T(8,128)S(1)} %dynamic_update_slice.7), channel_id=1, replica_groups=mesh['dom'=128,'blk'=4] {'blk'}, use_global_device_ids=true, to_apply=%region_12.13 | all-reduce | flops 2560 | bytes 15360 | tf_op jit(solution)/shard_map/psum | solution.py:98
  303.7 9.5 %psum.23 = f32[8]{0:T(128)} all-reduce(f32[8]{0:T(128)S(1)} %get-tuple-element.2), channel_id=1, replica_groups=mesh['dom'=128,'blk'=4] {'blk'}, use_global_device_ids=true, to_apply=%region_14.15 | all-reduce | flops 8 | bytes 64 | tf_op jit(solution)/shard_map/psum | solution.py:102
  (176 shorter events, 91.8 us)
Async XLA Ops:
  4.0 50.7 %collective-permute-start = (s32[4]{0:T(128)S(1)}, s32[4]{0:T(128)S(1)}, u32[]{:S(2)}, u32[]{:S(2)}) collective-permute-start(s32[4]{0:T(128)S(1)} %get-tuple-element.45), channel_id=1, source_target_pairs={{508,0},{0,4},{4,8},{8,12},{12,16},{16,20},{20,24},{24,28},{28,32}... | collective-permute-start | bytes 56 | tf_op jit(solution)/shard_map/ppermute | solution.py:14
  5.9 50.8 %collective-permute-start.1 = (s32[4]{0:T(128)S(1)}, s32[4]{0:T(128)S(1)}, u32[]{:S(2)}, u32[]{:S(2)}) collective-permute-start(s32[4]{0:T(128)S(1)} %get-tuple-element.44), channel_id=1, source_target_pairs={{504,0},{508,4},{0,8},{4,12},{8,16},{12,20},{16,24},{20,28},{24,32... | collective-permute-start | bytes 56 | tf_op jit(solution)/shard_map/ppermute | solution.py:14
  9.7 48.9 %collective-permute-start.2 = (s32[4]{0:T(128)S(1)}, s32[4]{0:T(128)S(1)}, u32[]{:S(2)}, u32[]{:S(2)}) collective-permute-start(s32[4]{0:T(128)S(1)} %get-tuple-element.43), channel_id=1, source_target_pairs={{500,0},{504,4},{508,8},{0,12},{4,16},{8,20},{12,24},{16,28},{20,3... | collective-permute-start | bytes 56 | tf_op jit(solution)/shard_map/ppermute | solution.py:14
  16.1 47.8 %collective-permute-start.3 = (s32[4]{0:T(128)S(1)}, s32[4]{0:T(128)S(1)}, u32[]{:S(2)}, u32[]{:S(2)}) collective-permute-start(s32[4]{0:T(128)S(1)} %get-tuple-element.42), channel_id=1, source_target_pairs={{496,0},{500,4},{504,8},{508,12},{0,16},{4,20},{8,24},{12,28},{16,... | collective-permute-start | bytes 56 | tf_op jit(solution)/shard_map/ppermute | solution.py:14
  21.3 46.1 %collective-permute-start.4 = (s32[4]{0:T(128)S(1)}, s32[4]{0:T(128)S(1)}, u32[]{:S(2)}, u32[]{:S(2)}) collective-permute-start(s32[4]{0:T(128)S(1)} %get-tuple-element.41), channel_id=1, source_target_pairs={{4,0},{8,4},{12,8},{16,12},{20,16},{24,20},{28,24},{32,28},{36,32}... | collective-permute-start | bytes 56 | tf_op jit(solution)/shard_map/ppermute | solution.py:14
  54.7 14.9 %collective-permute-start.5 = (s32[4]{0:T(128)S(1)}, s32[4]{0:T(128)S(1)}, u32[]{:S(2)}, u32[]{:S(2)}) collective-permute-start(s32[4]{0:T(128)S(1)} %get-tuple-element.40), channel_id=1, source_target_pairs={{8,0},{12,4},{16,8},{20,12},{24,16},{28,20},{32,24},{36,28},{40,32... | collective-permute-start | bytes 56 | tf_op jit(solution)/shard_map/ppermute | solution.py:14
  56.7 16.8 %collective-permute-start.6 = (s32[4]{0:T(128)S(1)}, s32[4]{0:T(128)S(1)}, u32[]{:S(2)}, u32[]{:S(2)}) collective-permute-start(s32[4]{0:T(128)S(1)} %get-tuple-element.39), channel_id=1, source_target_pairs={{12,0},{16,4},{20,8},{24,12},{28,16},{32,20},{36,24},{40,28},{44,3... | collective-permute-start | bytes 56 | tf_op jit(solution)/shard_map/ppermute | solution.py:14
  58.7 19.7 %collective-permute-start.7 = (s32[4]{0:T(128)S(1)}, s32[4]{0:T(128)S(1)}, u32[]{:S(2)}, u32[]{:S(2)}) collective-permute-start(s32[4]{0:T(128)S(1)} %get-tuple-element.38), channel_id=1, source_target_pairs={{16,0},{20,4},{24,8},{28,12},{32,16},{36,20},{40,24},{44,28},{48,3... | collective-permute-start | bytes 56 | tf_op jit(solution)/shard_map/ppermute | solution.py:14
  63.9 81.7 %collective-permute-start.8 = (f32[4,320]{1,0:T(4,128)S(1)}, f32[4,320]{1,0:T(4,128)S(1)}, u32[]{:S(2)}, u32[]{:S(2)}) collective-permute-start(f32[4,320]{1,0:T(4,128)S(1)} %get-tuple-element.21), channel_id=1, source_target_pairs={{508,0},{0,4},{4,8},{8,12},{12,16},{16,20},{20,24},{24,28},{28,32}... | collective-permute-start | bytes 15368 | tf_op jit(solution)/shard_map/ppermute | solution.py:14
  67.4 81.6 %collective-permute-start.9 = (f32[4,320]{1,0:T(4,128)S(1)}, f32[4,320]{1,0:T(4,128)S(1)}, u32[]{:S(2)}, u32[]{:S(2)}) collective-permute-start(f32[4,320]{1,0:T(4,128)S(1)} %get-tuple-element.20), channel_id=1, source_target_pairs={{504,0},{508,4},{0,8},{4,12},{8,16},{12,20},{16,24},{20,28},{24,32... | collective-permute-start | bytes 15368 | tf_op jit(solution)/shard_map/ppermute | solution.py:14
  69.6 86.2 %collective-permute-start.10 = (f32[4,320]{1,0:T(4,128)S(1)}, f32[4,320]{1,0:T(4,128)S(1)}, u32[]{:S(2)}, u32[]{:S(2)}) collective-permute-start(f32[4,320]{1,0:T(4,128)S(1)} %get-tuple-element.19), channel_id=1, source_target_pairs={{500,0},{504,4},{508,8},{0,12},{4,16},{8,20},{12,24},{16,28},{20,3... | collective-permute-start | bytes 15368 | tf_op jit(solution)/shard_map/ppermute | solution.py:14
  73.6 84.2 %collective-permute-start.11 = (f32[4,320]{1,0:T(4,128)S(1)}, f32[4,320]{1,0:T(4,128)S(1)}, u32[]{:S(2)}, u32[]{:S(2)}) collective-permute-start(f32[4,320]{1,0:T(4,128)S(1)} %get-tuple-element.18), channel_id=1, source_target_pairs={{496,0},{500,4},{504,8},{508,12},{0,16},{4,20},{8,24},{12,28},{16,... | collective-permute-start | bytes 15368 | tf_op jit(solution)/shard_map/ppermute | solution.py:14
  88.4 9.4 %collective-permute-start.18 = (bf16[4,320]{1,0:T(4,128)(2,1)S(1)}, bf16[4,320]{1,0:T(4,128)(2,1)S(1)}, u32[]{:S(2)}, u32[]{:S(2)}) collective-permute-start(bf16[4,320]{1,0:T(4,128)(2,1)S(1)} %get-tuple-element.35), channel_id=1, source_target_pairs={{12,0},{16,4},{20,8},{24,12},{28,16},{32,20},{36,24},{40,28},{44,3... | collective-permute-start | bytes 7688 | tf_op jit(solution)/shard_map/ppermute | solution.py:14
  97.8 7.6 %collective-permute-start.19 = (bf16[4,320]{1,0:T(4,128)(2,1)S(1)}, bf16[4,320]{1,0:T(4,128)(2,1)S(1)}, u32[]{:S(2)}, u32[]{:S(2)}) collective-permute-start(bf16[4,320]{1,0:T(4,128)(2,1)S(1)} %get-tuple-element.34), channel_id=1, source_target_pairs={{16,0},{20,4},{24,8},{28,12},{32,16},{36,20},{40,24},{44,28},{48,3... | collective-permute-start | bytes 7688 | tf_op jit(solution)/shard_map/ppermute | solution.py:14
  105.4 9.2 %collective-permute-start.20 = (bf16[4,320]{1,0:T(4,128)(2,1)S(1)}, bf16[4,320]{1,0:T(4,128)(2,1)S(1)}, u32[]{:S(2)}, u32[]{:S(2)}) collective-permute-start(bf16[4,320]{1,0:T(4,128)(2,1)S(1)} %get-tuple-element.33), channel_id=1, source_target_pairs={{508,0},{0,4},{4,8},{8,12},{12,16},{16,20},{20,24},{24,28},{28,32}... | collective-permute-start | bytes 7688 | tf_op jit(solution)/shard_map/ppermute | solution.py:14
  126.4 15.7 %collective-permute-start.23 = (bf16[4,320]{1,0:T(4,128)(2,1)S(1)}, bf16[4,320]{1,0:T(4,128)(2,1)S(1)}, u32[]{:S(2)}, u32[]{:S(2)}) collective-permute-start(bf16[4,320]{1,0:T(4,128)(2,1)S(1)} %get-tuple-element.30), channel_id=1, source_target_pairs={{496,0},{500,4},{504,8},{508,12},{0,16},{4,20},{8,24},{12,28},{16,... | collective-permute-start | bytes 7688 | tf_op jit(solution)/shard_map/ppermute | solution.py:14
  142.2 15.6 %collective-permute-start.12 = (f32[4,320]{1,0:T(4,128)S(1)}, f32[4,320]{1,0:T(4,128)S(1)}, u32[]{:S(2)}, u32[]{:S(2)}) collective-permute-start(f32[4,320]{1,0:T(4,128)S(1)} %get-tuple-element.17), channel_id=1, source_target_pairs={{4,0},{8,4},{12,8},{16,12},{20,16},{24,20},{28,24},{32,28},{36,32}... | collective-permute-start | bytes 15368 | tf_op jit(solution)/shard_map/ppermute | solution.py:14
  145.6 12.2 %collective-permute-start.13 = (f32[4,320]{1,0:T(4,128)S(1)}, f32[4,320]{1,0:T(4,128)S(1)}, u32[]{:S(2)}, u32[]{:S(2)}) collective-permute-start(f32[4,320]{1,0:T(4,128)S(1)} %get-tuple-element.16), channel_id=1, source_target_pairs={{8,0},{12,4},{16,8},{20,12},{24,16},{28,20},{32,24},{36,28},{40,32... | collective-permute-start | bytes 15368 | tf_op jit(solution)/shard_map/ppermute | solution.py:14
  149.0 8.8 %collective-permute-start.14 = (f32[4,320]{1,0:T(4,128)S(1)}, f32[4,320]{1,0:T(4,128)S(1)}, u32[]{:S(2)}, u32[]{:S(2)}) collective-permute-start(f32[4,320]{1,0:T(4,128)S(1)} %get-tuple-element.15), channel_id=1, source_target_pairs={{12,0},{16,4},{20,8},{24,12},{28,16},{32,20},{36,24},{40,28},{44,3... | collective-permute-start | bytes 15368 | tf_op jit(solution)/shard_map/ppermute | solution.py:14
  155.9 7.6 %collective-permute-start.15 = (f32[4,320]{1,0:T(4,128)S(1)}, f32[4,320]{1,0:T(4,128)S(1)}, u32[]{:S(2)}, u32[]{:S(2)}) collective-permute-start(f32[4,320]{1,0:T(4,128)S(1)} %get-tuple-element.14), channel_id=1, source_target_pairs={{16,0},{20,4},{24,8},{28,12},{32,16},{36,20},{40,24},{44,28},{48,3... | collective-permute-start | bytes 15368 | tf_op jit(solution)/shard_map/ppermute | solution.py:14
  194.6 13.3 %collective-permute-start.32 = (bf16[4,320]{1,0:T(4,128)(2,1)S(1)}, bf16[4,320]{1,0:T(4,128)(2,1)S(1)}, u32[]{:S(2)}, u32[]{:S(2)}) collective-permute-start(bf16[4,320]{1,0:T(4,128)(2,1)S(1)} %get-tuple-element.29), channel_id=1, source_target_pairs={{4,0},{8,4},{12,8},{16,12},{20,16},{24,20},{28,24},{32,28},{36,32}... | collective-permute-start | bytes 7688 | tf_op jit(solution)/shard_map/ppermute | solution.py:14
  198.0 70.4 %collective-permute-start.24 = (f32[4,320]{1,0:T(4,128)S(1)}, f32[4,320]{1,0:T(4,128)S(1)}, u32[]{:S(2)}, u32[]{:S(2)}) collective-permute-start(f32[4,320]{1,0:T(4,128)S(1)} %get-tuple-element.13), channel_id=1, source_target_pairs={{508,0},{0,4},{4,8},{8,12},{12,16},{16,20},{20,24},{24,28},{28,32}... | collective-permute-start | bytes 15368 | tf_op jit(solution)/shard_map/ppermute | solution.py:14
  200.5 71.4 %collective-permute-start.25 = (f32[4,320]{1,0:T(4,128)S(1)}, f32[4,320]{1,0:T(4,128)S(1)}, u32[]{:S(2)}, u32[]{:S(2)}) collective-permute-start(f32[4,320]{1,0:T(4,128)S(1)} %get-tuple-element.12), channel_id=1, source_target_pairs={{504,0},{508,4},{0,8},{4,12},{8,16},{12,20},{16,24},{20,28},{24,32... | collective-permute-start | bytes 15368 | tf_op jit(solution)/shard_map/ppermute | solution.py:14
  204.1 74.6 %collective-permute-start.26 = (f32[4,320]{1,0:T(4,128)S(1)}, f32[4,320]{1,0:T(4,128)S(1)}, u32[]{:S(2)}, u32[]{:S(2)}) collective-permute-start(f32[4,320]{1,0:T(4,128)S(1)} %get-tuple-element.11), channel_id=1, source_target_pairs={{500,0},{504,4},{508,8},{0,12},{4,16},{8,20},{12,24},{16,28},{20,3... | collective-permute-start | bytes 15368 | tf_op jit(solution)/shard_map/ppermute | solution.py:14
  206.0 74.6 %collective-permute-start.27 = (f32[4,320]{1,0:T(4,128)S(1)}, f32[4,320]{1,0:T(4,128)S(1)}, u32[]{:S(2)}, u32[]{:S(2)}) collective-permute-start(f32[4,320]{1,0:T(4,128)S(1)} %get-tuple-element.10), channel_id=1, source_target_pairs={{496,0},{500,4},{504,8},{508,12},{0,16},{4,20},{8,24},{12,28},{16,... | collective-permute-start | bytes 15368 | tf_op jit(solution)/shard_map/ppermute | solution.py:14
  220.7 7.6 %collective-permute-start.35 = (bf16[4,320]{1,0:T(4,128)(2,1)S(1)}, bf16[4,320]{1,0:T(4,128)(2,1)S(1)}, u32[]{:S(2)}, u32[]{:S(2)}) collective-permute-start(bf16[4,320]{1,0:T(4,128)(2,1)S(1)} %get-tuple-element.26), channel_id=1, source_target_pairs={{16,0},{20,4},{24,8},{28,12},{32,16},{36,20},{40,24},{44,28},{48,3... | collective-permute-start | bytes 7688 | tf_op jit(solution)/shard_map/ppermute | solution.py:14
  228.3 9.2 %collective-permute-start.36 = (bf16[4,320]{1,0:T(4,128)(2,1)S(1)}, bf16[4,320]{1,0:T(4,128)(2,1)S(1)}, u32[]{:S(2)}, u32[]{:S(2)}) collective-permute-start(bf16[4,320]{1,0:T(4,128)(2,1)S(1)} %get-tuple-element.25), channel_id=1, source_target_pairs={{508,0},{0,4},{4,8},{8,12},{12,16},{16,20},{20,24},{24,28},{28,32}... | collective-permute-start | bytes 7688 | tf_op jit(solution)/shard_map/ppermute | solution.py:14
  250.7 14.3 %collective-permute-start.39 = (bf16[4,320]{1,0:T(4,128)(2,1)S(1)}, bf16[4,320]{1,0:T(4,128)(2,1)S(1)}, u32[]{:S(2)}, u32[]{:S(2)}) collective-permute-start(bf16[4,320]{1,0:T(4,128)(2,1)S(1)} %get-tuple-element.22), channel_id=1, source_target_pairs={{496,0},{500,4},{504,8},{508,12},{0,16},{4,20},{8,24},{12,28},{16,... | collective-permute-start | bytes 7688 | tf_op jit(solution)/shard_map/ppermute | solution.py:14
  265.0 15.6 %collective-permute-start.28 = (f32[4,320]{1,0:T(4,128)S(1)}, f32[4,320]{1,0:T(4,128)S(1)}, u32[]{:S(2)}, u32[]{:S(2)}) collective-permute-start(f32[4,320]{1,0:T(4,128)S(1)} %get-tuple-element.9), channel_id=1, source_target_pairs={{4,0},{8,4},{12,8},{16,12},{20,16},{24,20},{28,24},{32,28},{36,32}... | collective-permute-start | bytes 15368 | tf_op jit(solution)/shard_map/ppermute | solution.py:14
  268.4 12.2 %collective-permute-start.29 = (f32[4,320]{1,0:T(4,128)S(1)}, f32[4,320]{1,0:T(4,128)S(1)}, u32[]{:S(2)}, u32[]{:S(2)}) collective-permute-start(f32[4,320]{1,0:T(4,128)S(1)} %get-tuple-element.8), channel_id=1, source_target_pairs={{8,0},{12,4},{16,8},{20,12},{24,16},{28,20},{32,24},{36,28},{40,32... | collective-permute-start | bytes 15368 | tf_op jit(solution)/shard_map/ppermute | solution.py:14
  271.9 8.8 %collective-permute-start.30 = (f32[4,320]{1,0:T(4,128)S(1)}, f32[4,320]{1,0:T(4,128)S(1)}, u32[]{:S(2)}, u32[]{:S(2)}) collective-permute-start(f32[4,320]{1,0:T(4,128)S(1)} %get-tuple-element.7), channel_id=1, source_target_pairs={{12,0},{16,4},{20,8},{24,12},{28,16},{32,20},{36,24},{40,28},{44,3... | collective-permute-start | bytes 15368 | tf_op jit(solution)/shard_map/ppermute | solution.py:14
  278.7 7.6 %collective-permute-start.31 = (f32[4,320]{1,0:T(4,128)S(1)}, f32[4,320]{1,0:T(4,128)S(1)}, u32[]{:S(2)}, u32[]{:S(2)}) collective-permute-start(f32[4,320]{1,0:T(4,128)S(1)} %get-tuple-element.6), channel_id=1, source_target_pairs={{16,0},{20,4},{24,8},{28,12},{32,16},{36,20},{40,24},{44,28},{48,3... | collective-permute-start | bytes 15368 | tf_op jit(solution)/shard_map/ppermute | solution.py:14
  (12 other events, 261.7 us)
where the time goes:
time: 315 us; the launch traced here: 313 us
  starting transfers between devices  130 us (41%)
  waiting for transfers between devices  83.1 us (26%)
  blocking collectives  71.8 us (23%)
  other arithmetic  13.5 us (4%)
  local copies, waits for them, and re-layouts  8.94 us (3%)
  matrix products  4.21 us (1%)
    ppermute x40, starting transfers between devices, from_behind(): return lax.ppermute(block, axis, route)  130 us
    ppermute x40, waiting for transfers between devices, from_behind(): return lax.ppermute(block, axis, route)  83.1 us
    all_gather x3, blocking collectives, full_rows(): return lax.all_gather(values, 'blk', axis=1, tiled=True)  32.2 us
    psum x2, blocking collectives, local(): summed = lax.psum(partial_value, 'blk')  30.1 us
    psum x1, blocking collectives, local(): indicator = lax.psum(weights, 'blk')  9.47 us
  transfers between devices with their start and end apart: 40, of which 17 were waited for; matrix products, arithmetic and copies ran while one was open for 5% of the time, Pallas kernels for 0%

commit v1 on v0

--- a/solution.py
+++ b/solution.py
@@ -15,7 +15,7 @@
 
 
 def full_rows(values):
-    return lax.all_gather(values, "blk", axis=1, tiled=True)
+    return jnp.concatenate(lax.all_gather(values, "blk"), axis=1)
 
 
 def local(degree, face_elem, face_side, face_peer, coupling, inv_diag, inv_off, source, residual):

time: 315 us -> 314 us (level)
  no operation moved by 1% of the time
where the time goes in v1:
time: 314 us; the launch traced here: 313 us
  starting transfers between devices  130 us (41%)
  waiting for transfers between devices  83.1 us (26%)
  blocking collectives  71.7 us (23%)
  other arithmetic  12.8 us (4%)
  local copies, waits for them, and re-layouts  9.03 us (3%)
  matrix products  4.21 us (1%)
    ppermute x40, starting transfers between devices, from_behind(): return lax.ppermute(block, axis, route)  130 us
    ppermute x40, waiting for transfers between devices, from_behind(): return lax.ppermute(block, axis, route)  83.1 us
    all_gather x3, blocking collectives, full_rows(): return jnp.concatenate(lax.all_gather(values, 'blk'), axis=1)  32.2 us
    psum x2, blocking collectives, local(): summed = lax.psum(partial_value, 'blk')  30.1 us
    psum x1, blocking collectives, local(): indicator = lax.psum(weights, 'blk')  9.47 us
  transfers between devices with their start and end apart: 40, of which 17 were waited for; matrix products, arithmetic and copies ran while one was open for 5% of the time, Pallas kernels for 0%

profile of v1, /device:TPU:64, one launch (start us, length us, event | category | flops | bytes accessed | tf_op | source)
XLA Modules:
  0.0 312.6 jit_solution(11335333235190075278)
XLA Ops:
  5.9 3.8 %collective-permute-start.1 = (s32[4]{0:T(128)S(1)}, s32[4]{0:T(128)S(1)}, u32[]{:S(2)}, u32[]{:S(2)}) collective-permute-start(s32[4]{0:T(128)S(1)} %get-tuple-element.44), channel_id=1, source_target_pairs={{504,0},{508,4},{0,8},{4,12},{8,16},{12,20},{16,24},{20,28},{24,32... | collective-permute-start | bytes 56 | tf_op jit(solution)/shard_map/ppermute | solution.py:14
  9.7 6.4 %collective-permute-start.2 = (s32[4]{0:T(128)S(1)}, s32[4]{0:T(128)S(1)}, u32[]{:S(2)}, u32[]{:S(2)}) collective-permute-start(s32[4]{0:T(128)S(1)} %get-tuple-element.43), channel_id=1, source_target_pairs={{500,0},{504,4},{508,8},{0,12},{4,16},{8,20},{12,24},{16,28},{20,3... | collective-permute-start | bytes 56 | tf_op jit(solution)/shard_map/ppermute | solution.py:14
  16.1 5.2 %collective-permute-start.3 = (s32[4]{0:T(128)S(1)}, s32[4]{0:T(128)S(1)}, u32[]{:S(2)}, u32[]{:S(2)}) collective-permute-start(s32[4]{0:T(128)S(1)} %get-tuple-element.42), channel_id=1, source_target_pairs={{496,0},{500,4},{504,8},{508,12},{0,16},{4,20},{8,24},{12,28},{16,... | collective-permute-start | bytes 56 | tf_op jit(solution)/shard_map/ppermute | solution.py:14
  25.4 11.3 %all-gather = bf16[32,80]{1,0:T(8,128)(2,1)S(1)} all-gather(bf16[8,80]{1,0:T(8,128)(2,1)S(1)} %fusion.30), channel_id=2, replica_groups=mesh['dom'=128,'blk'=4] {'blk'}, dimensions={0}, use_global_device_ids=true | all-gather | bytes 6400 | tf_op jit(solution)/shard_map/all_gather | solution.py:18
  40.3 10.4 %all-gather.1 = bf16[32,80]{1,0:T(8,128)(2,1)S(1)} all-gather(bf16[8,80]{1,0:T(8,128)(2,1)S(1)} %fusion.40), channel_id=3, replica_groups=mesh['dom'=128,'blk'=4] {'blk'}, dimensions={0}, use_global_device_ids=true | all-gather | bytes 6400 | tf_op jit(solution)/shard_map/all_gather | solution.py:18
  58.1 5.2 %collective-permute-start.7 = (s32[4]{0:T(128)S(1)}, s32[4]{0:T(128)S(1)}, u32[]{:S(2)}, u32[]{:S(2)}) collective-permute-start(s32[4]{0:T(128)S(1)} %get-tuple-element.38), channel_id=1, source_target_pairs={{16,0},{20,4},{24,8},{28,12},{32,16},{36,20},{40,24},{44,28},{48,3... | collective-permute-start | bytes 56 | tf_op jit(solution)/shard_map/ppermute | solution.py:14
  63.4 3.5 %collective-permute-start.8 = (f32[4,320]{1,0:T(4,128)S(1)}, f32[4,320]{1,0:T(4,128)S(1)}, u32[]{:S(2)}, u32[]{:S(2)}) collective-permute-start(f32[4,320]{1,0:T(4,128)S(1)} %get-tuple-element.21), channel_id=1, source_target_pairs={{508,0},{0,4},{4,8},{8,12},{12,16},{16,20},{20,24},{24,28},{28,32}... | collective-permute-start | bytes 15368 | tf_op jit(solution)/shard_map/ppermute | solution.py:14
  69.1 3.9 %collective-permute-start.10 = (f32[4,320]{1,0:T(4,128)S(1)}, f32[4,320]{1,0:T(4,128)S(1)}, u32[]{:S(2)}, u32[]{:S(2)}) collective-permute-start(f32[4,320]{1,0:T(4,128)S(1)} %get-tuple-element.19), channel_id=1, source_target_pairs={{500,0},{504,4},{508,8},{0,12},{4,16},{8,20},{12,24},{16,28},{20,3... | collective-permute-start | bytes 15368 | tf_op jit(solution)/shard_map/ppermute | solution.py:14
  73.0 4.8 %collective-permute-start.11 = (f32[4,320]{1,0:T(4,128)S(1)}, f32[4,320]{1,0:T(4,128)S(1)}, u32[]{:S(2)}, u32[]{:S(2)}) collective-permute-start(f32[4,320]{1,0:T(4,128)S(1)} %get-tuple-element.18), channel_id=1, source_target_pairs={{496,0},{500,4},{504,8},{508,12},{0,16},{4,20},{8,24},{12,28},{16,... | collective-permute-start | bytes 15368 | tf_op jit(solution)/shard_map/ppermute | solution.py:14
  87.9 8.1 %collective-permute-start.18 = (bf16[4,320]{1,0:T(4,128)(2,1)S(1)}, bf16[4,320]{1,0:T(4,128)(2,1)S(1)}, u32[]{:S(2)}, u32[]{:S(2)}) collective-permute-start(bf16[4,320]{1,0:T(4,128)(2,1)S(1)} %get-tuple-element.35), channel_id=1, source_target_pairs={{12,0},{16,4},{20,8},{24,12},{28,16},{32,20},{36,24},{40,28},{44,3... | collective-permute-start | bytes 7688 | tf_op jit(solution)/shard_map/ppermute | solution.py:14
  97.3 3.6 %collective-permute-start.19 = (bf16[4,320]{1,0:T(4,128)(2,1)S(1)}, bf16[4,320]{1,0:T(4,128)(2,1)S(1)}, u32[]{:S(2)}, u32[]{:S(2)}) collective-permute-start(bf16[4,320]{1,0:T(4,128)(2,1)S(1)} %get-tuple-element.34), channel_id=1, source_target_pairs={{16,0},{20,4},{24,8},{28,12},{32,16},{36,20},{40,24},{44,28},{48,3... | collective-permute-start | bytes 7688 | tf_op jit(solution)/shard_map/ppermute | solution.py:14
  100.9 4.0 %collective-permute-done.19 = bf16[4,320]{1,0:T(4,128)(2,1)S(1)} collective-permute-done((bf16[4,320]{1,0:T(4,128)(2,1)S(1)}, bf16[4,320]{1,0:T(4,128)(2,1)S(1)}, u32[]{:S(2)}, u32[]{:S(2)}) %collective-permute-start.19) | collective-permute-done | bytes 2592 | tf_op jit(solution)/shard_map/ppermute | solution.py:14
  106.8 7.2 %collective-permute-done.20 = bf16[4,320]{1,0:T(4,128)(2,1)S(1)} collective-permute-done((bf16[4,320]{1,0:T(4,128)(2,1)S(1)}, bf16[4,320]{1,0:T(4,128)(2,1)S(1)}, u32[]{:S(2)}, u32[]{:S(2)}) %collective-permute-start.20) | collective-permute-done | bytes 2592 | tf_op jit(solution)/shard_map/ppermute | solution.py:14
  116.0 3.5 %collective-permute-done.21 = bf16[4,320]{1,0:T(4,128)(2,1)S(1)} collective-permute-done((bf16[4,320]{1,0:T(4,128)(2,1)S(1)}, bf16[4,320]{1,0:T(4,128)(2,1)S(1)}, u32[]{:S(2)}, u32[]{:S(2)}) %collective-permute-start.21) | collective-permute-done | bytes 2592 | tf_op jit(solution)/shard_map/ppermute | solution.py:14
  121.4 4.4 %collective-permute-done.22 = bf16[4,320]{1,0:T(4,128)(2,1)S(1)} collective-permute-done((bf16[4,320]{1,0:T(4,128)(2,1)S(1)}, bf16[4,320]{1,0:T(4,128)(2,1)S(1)}, u32[]{:S(2)}, u32[]{:S(2)}) %collective-permute-start.22) | collective-permute-done | bytes 2592 | tf_op jit(solution)/shard_map/ppermute | solution.py:14
  128.0 13.6 %collective-permute-done.23 = bf16[4,320]{1,0:T(4,128)(2,1)S(1)} collective-permute-done((bf16[4,320]{1,0:T(4,128)(2,1)S(1)}, bf16[4,320]{1,0:T(4,128)(2,1)S(1)}, u32[]{:S(2)}, u32[]{:S(2)}) %collective-permute-start.23) | collective-permute-done | bytes 2592 | tf_op jit(solution)/shard_map/ppermute | solution.py:14
  145.1 3.4 %collective-permute-start.13 = (f32[4,320]{1,0:T(4,128)S(1)}, f32[4,320]{1,0:T(4,128)S(1)}, u32[]{:S(2)}, u32[]{:S(2)}) collective-permute-start(f32[4,320]{1,0:T(4,128)S(1)} %get-tuple-element.16), channel_id=1, source_target_pairs={{8,0},{12,4},{16,8},{20,12},{24,16},{28,20},{32,24},{36,28},{40,32... | collective-permute-start | bytes 15368 | tf_op jit(solution)/shard_map/ppermute | solution.py:14
  148.5 6.8 %collective-permute-start.14 = (f32[4,320]{1,0:T(4,128)S(1)}, f32[4,320]{1,0:T(4,128)S(1)}, u32[]{:S(2)}, u32[]{:S(2)}) collective-permute-start(f32[4,320]{1,0:T(4,128)S(1)} %get-tuple-element.15), channel_id=1, source_target_pairs={{12,0},{16,4},{20,8},{24,12},{28,16},{32,20},{36,24},{40,28},{44,3... | collective-permute-start | bytes 15368 | tf_op jit(solution)/shard_map/ppermute | solution.py:14
  157.3 5.6 %collective-permute-done.15 = f32[4,320]{1,0:T(4,128)S(1)} collective-permute-done((f32[4,320]{1,0:T(4,128)S(1)}, f32[4,320]{1,0:T(4,128)S(1)}, u32[]{:S(2)}, u32[]{:S(2)}) %collective-permute-start.15) | collective-permute-done | bytes 5152 | tf_op jit(solution)/shard_map/ppermute | solution.py:14
  164.8 15.8 %psum.21 = bf16[8,320]{1,0:T(8,128)(2,1)S(1)} all-reduce(f32[8,320]{1,0:T(8,128)S(1)} %dynamic_update_slice.6), channel_id=1, replica_groups=mesh['dom'=128,'blk'=4] {'blk'}, use_global_device_ids=true, to_apply=%region_7.8 | all-reduce | flops 2560 | bytes 15360 | tf_op jit(solution)/shard_map/psum | solution.py:98
  181.7 10.4 %all-gather.2 = bf16[32,80]{1,0:T(8,128)(2,1)S(1)} all-gather(bf16[8,80]{1,0:T(8,128)(2,1)S(1)} %fusion.31), channel_id=4, replica_groups=mesh['dom'=128,'blk'=4] {'blk'}, dimensions={0}, use_global_device_ids=true | all-gather | bytes 6400 | tf_op jit(solution)/shard_map/all_gather | solution.py:18
  199.9 3.6 %collective-permute-start.25 = (f32[4,320]{1,0:T(4,128)S(1)}, f32[4,320]{1,0:T(4,128)S(1)}, u32[]{:S(2)}, u32[]{:S(2)}) collective-permute-start(f32[4,320]{1,0:T(4,128)S(1)} %get-tuple-element.12), channel_id=1, source_target_pairs={{504,0},{508,4},{0,8},{4,12},{8,16},{12,20},{16,24},{20,28},{24,32... | collective-permute-start | bytes 15368 | tf_op jit(solution)/shard_map/ppermute | solution.py:14
  212.9 5.9 %collective-permute-start.34 = (bf16[4,320]{1,0:T(4,128)(2,1)S(1)}, bf16[4,320]{1,0:T(4,128)(2,1)S(1)}, u32[]{:S(2)}, u32[]{:S(2)}) collective-permute-start(bf16[4,320]{1,0:T(4,128)(2,1)S(1)} %get-tuple-element.27), channel_id=1, source_target_pairs={{12,0},{16,4},{20,8},{24,12},{28,16},{32,20},{36,24},{40,28},{44,3... | collective-permute-start | bytes 7688 | tf_op jit(solution)/shard_map/ppermute | solution.py:14
  220.1 5.3 %collective-permute-start.35 = (bf16[4,320]{1,0:T(4,128)(2,1)S(1)}, bf16[4,320]{1,0:T(4,128)(2,1)S(1)}, u32[]{:S(2)}, u32[]{:S(2)}) collective-permute-start(bf16[4,320]{1,0:T(4,128)(2,1)S(1)} %get-tuple-element.26), channel_id=1, source_target_pairs={{16,0},{20,4},{24,8},{28,12},{32,16},{36,20},{40,24},{44,28},{48,3... | collective-permute-start | bytes 7688 | tf_op jit(solution)/shard_map/ppermute | solution.py:14
  230.8 6.0 %collective-permute-done.36 = bf16[4,320]{1,0:T(4,128)(2,1)S(1)} collective-permute-done((bf16[4,320]{1,0:T(4,128)(2,1)S(1)}, bf16[4,320]{1,0:T(4,128)(2,1)S(1)}, u32[]{:S(2)}, u32[]{:S(2)}) %collective-permute-start.36) | collective-permute-done | bytes 2592 | tf_op jit(solution)/shard_map/ppermute | solution.py:14
  238.8 4.8 %collective-permute-done.37 = bf16[4,320]{1,0:T(4,128)(2,1)S(1)} collective-permute-done((bf16[4,320]{1,0:T(4,128)(2,1)S(1)}, bf16[4,320]{1,0:T(4,128)(2,1)S(1)}, u32[]{:S(2)}, u32[]{:S(2)}) %collective-permute-start.37) | collective-permute-done | bytes 2592 | tf_op jit(solution)/shard_map/ppermute | solution.py:14
  245.5 4.6 %collective-permute-done.38 = bf16[4,320]{1,0:T(4,128)(2,1)S(1)} collective-permute-done((bf16[4,320]{1,0:T(4,128)(2,1)S(1)}, bf16[4,320]{1,0:T(4,128)(2,1)S(1)}, u32[]{:S(2)}, u32[]{:S(2)}) %collective-permute-start.38) | collective-permute-done | bytes 2592 | tf_op jit(solution)/shard_map/ppermute | solution.py:14
  252.1 12.3 %collective-permute-done.39 = bf16[4,320]{1,0:T(4,128)(2,1)S(1)} collective-permute-done((bf16[4,320]{1,0:T(4,128)(2,1)S(1)}, bf16[4,320]{1,0:T(4,128)(2,1)S(1)}, u32[]{:S(2)}, u32[]{:S(2)}) %collective-permute-start.39) | collective-permute-done | bytes 2592 | tf_op jit(solution)/shard_map/ppermute | solution.py:14
  271.3 6.8 %collective-permute-start.30 = (f32[4,320]{1,0:T(4,128)S(1)}, f32[4,320]{1,0:T(4,128)S(1)}, u32[]{:S(2)}, u32[]{:S(2)}) collective-permute-start(f32[4,320]{1,0:T(4,128)S(1)} %get-tuple-element.7), channel_id=1, source_target_pairs={{12,0},{16,4},{20,8},{24,12},{28,16},{32,20},{36,24},{40,28},{44,3... | collective-permute-start | bytes 15368 | tf_op jit(solution)/shard_map/ppermute | solution.py:14
  280.2 5.6 %collective-permute-done.31 = f32[4,320]{1,0:T(4,128)S(1)} collective-permute-done((f32[4,320]{1,0:T(4,128)S(1)}, f32[4,320]{1,0:T(4,128)S(1)}, u32[]{:S(2)}, u32[]{:S(2)}) %collective-permute-start.31) | collective-permute-done | bytes 5152 | tf_op jit(solution)/shard_map/ppermute | solution.py:14
  287.7 14.3 %psum.22 = bf16[8,320]{1,0:T(8,128)(2,1)S(1)} all-reduce(f32[8,320]{1,0:T(8,128)S(1)} %dynamic_update_slice.7), channel_id=1, replica_groups=mesh['dom'=128,'blk'=4] {'blk'}, use_global_device_ids=true, to_apply=%region_12.13 | all-reduce | flops 2560 | bytes 15360 | tf_op jit(solution)/shard_map/psum | solution.py:98
  303.2 9.5 %psum.23 = f32[8]{0:T(128)} all-reduce(f32[8]{0:T(128)S(1)} %get-tuple-element.2), channel_id=1, replica_groups=mesh['dom'=128,'blk'=4] {'blk'}, use_global_device_ids=true, to_apply=%region_14.15 | all-reduce | flops 8 | bytes 64 | tf_op jit(solution)/shard_map/psum | solution.py:102
  (176 shorter events, 91.3 us)
Async XLA Ops:
  4.0 50.2 %collective-permute-start = (s32[4]{0:T(128)S(1)}, s32[4]{0:T(128)S(1)}, u32[]{:S(2)}, u32[]{:S(2)}) collective-permute-start(s32[4]{0:T(128)S(1)} %get-tuple-element.45), channel_id=1, source_target_pairs={{508,0},{0,4},{4,8},{8,12},{12,16},{16,20},{20,24},{24,28},{28,32}... | collective-permute-start | bytes 56 | tf_op jit(solution)/shard_map/ppermute | solution.py:14
  5.9 50.3 %collective-permute-start.1 = (s32[4]{0:T(128)S(1)}, s32[4]{0:T(128)S(1)}, u32[]{:S(2)}, u32[]{:S(2)}) collective-permute-start(s32[4]{0:T(128)S(1)} %get-tuple-element.44), channel_id=1, source_target_pairs={{504,0},{508,4},{0,8},{4,12},{8,16},{12,20},{16,24},{20,28},{24,32... | collective-permute-start | bytes 56 | tf_op jit(solution)/shard_map/ppermute | solution.py:14
  9.7 48.4 %collective-permute-start.2 = (s32[4]{0:T(128)S(1)}, s32[4]{0:T(128)S(1)}, u32[]{:S(2)}, u32[]{:S(2)}) collective-permute-start(s32[4]{0:T(128)S(1)} %get-tuple-element.43), channel_id=1, source_target_pairs={{500,0},{504,4},{508,8},{0,12},{4,16},{8,20},{12,24},{16,28},{20,3... | collective-permute-start | bytes 56 | tf_op jit(solution)/shard_map/ppermute | solution.py:14
  16.1 47.3 %collective-permute-start.3 = (s32[4]{0:T(128)S(1)}, s32[4]{0:T(128)S(1)}, u32[]{:S(2)}, u32[]{:S(2)}) collective-permute-start(s32[4]{0:T(128)S(1)} %get-tuple-element.42), channel_id=1, source_target_pairs={{496,0},{500,4},{504,8},{508,12},{0,16},{4,20},{8,24},{12,28},{16,... | collective-permute-start | bytes 56 | tf_op jit(solution)/shard_map/ppermute | solution.py:14
  21.3 45.5 %collective-permute-start.4 = (s32[4]{0:T(128)S(1)}, s32[4]{0:T(128)S(1)}, u32[]{:S(2)}, u32[]{:S(2)}) collective-permute-start(s32[4]{0:T(128)S(1)} %get-tuple-element.41), channel_id=1, source_target_pairs={{4,0},{8,4},{12,8},{16,12},{20,16},{24,20},{28,24},{32,28},{36,32}... | collective-permute-start | bytes 56 | tf_op jit(solution)/shard_map/ppermute | solution.py:14
  54.2 14.9 %collective-permute-start.5 = (s32[4]{0:T(128)S(1)}, s32[4]{0:T(128)S(1)}, u32[]{:S(2)}, u32[]{:S(2)}) collective-permute-start(s32[4]{0:T(128)S(1)} %get-tuple-element.40), channel_id=1, source_target_pairs={{8,0},{12,4},{16,8},{20,12},{24,16},{28,20},{32,24},{36,28},{40,32... | collective-permute-start | bytes 56 | tf_op jit(solution)/shard_map/ppermute | solution.py:14
  56.2 16.8 %collective-permute-start.6 = (s32[4]{0:T(128)S(1)}, s32[4]{0:T(128)S(1)}, u32[]{:S(2)}, u32[]{:S(2)}) collective-permute-start(s32[4]{0:T(128)S(1)} %get-tuple-element.39), channel_id=1, source_target_pairs={{12,0},{16,4},{20,8},{24,12},{28,16},{32,20},{36,24},{40,28},{44,3... | collective-permute-start | bytes 56 | tf_op jit(solution)/shard_map/ppermute | solution.py:14
  58.1 19.7 %collective-permute-start.7 = (s32[4]{0:T(128)S(1)}, s32[4]{0:T(128)S(1)}, u32[]{:S(2)}, u32[]{:S(2)}) collective-permute-start(s32[4]{0:T(128)S(1)} %get-tuple-element.38), channel_id=1, source_target_pairs={{16,0},{20,4},{24,8},{28,12},{32,16},{36,20},{40,24},{44,28},{48,3... | collective-permute-start | bytes 56 | tf_op jit(solution)/shard_map/ppermute | solution.py:14
  63.4 81.7 %collective-permute-start.8 = (f32[4,320]{1,0:T(4,128)S(1)}, f32[4,320]{1,0:T(4,128)S(1)}, u32[]{:S(2)}, u32[]{:S(2)}) collective-permute-start(f32[4,320]{1,0:T(4,128)S(1)} %get-tuple-element.21), channel_id=1, source_target_pairs={{508,0},{0,4},{4,8},{8,12},{12,16},{16,20},{20,24},{24,28},{28,32}... | collective-permute-start | bytes 15368 | tf_op jit(solution)/shard_map/ppermute | solution.py:14
  66.9 81.6 %collective-permute-start.9 = (f32[4,320]{1,0:T(4,128)S(1)}, f32[4,320]{1,0:T(4,128)S(1)}, u32[]{:S(2)}, u32[]{:S(2)}) collective-permute-start(f32[4,320]{1,0:T(4,128)S(1)} %get-tuple-element.20), channel_id=1, source_target_pairs={{504,0},{508,4},{0,8},{4,12},{8,16},{12,20},{16,24},{20,28},{24,32... | collective-permute-start | bytes 15368 | tf_op jit(solution)/shard_map/ppermute | solution.py:14
  69.1 86.2 %collective-permute-start.10 = (f32[4,320]{1,0:T(4,128)S(1)}, f32[4,320]{1,0:T(4,128)S(1)}, u32[]{:S(2)}, u32[]{:S(2)}) collective-permute-start(f32[4,320]{1,0:T(4,128)S(1)} %get-tuple-element.19), channel_id=1, source_target_pairs={{500,0},{504,4},{508,8},{0,12},{4,16},{8,20},{12,24},{16,28},{20,3... | collective-permute-start | bytes 15368 | tf_op jit(solution)/shard_map/ppermute | solution.py:14
  73.0 84.2 %collective-permute-start.11 = (f32[4,320]{1,0:T(4,128)S(1)}, f32[4,320]{1,0:T(4,128)S(1)}, u32[]{:S(2)}, u32[]{:S(2)}) collective-permute-start(f32[4,320]{1,0:T(4,128)S(1)} %get-tuple-element.18), channel_id=1, source_target_pairs={{496,0},{500,4},{504,8},{508,12},{0,16},{4,20},{8,24},{12,28},{16,... | collective-permute-start | bytes 15368 | tf_op jit(solution)/shard_map/ppermute | solution.py:14
  87.9 9.4 %collective-permute-start.18 = (bf16[4,320]{1,0:T(4,128)(2,1)S(1)}, bf16[4,320]{1,0:T(4,128)(2,1)S(1)}, u32[]{:S(2)}, u32[]{:S(2)}) collective-permute-start(bf16[4,320]{1,0:T(4,128)(2,1)S(1)} %get-tuple-element.35), channel_id=1, source_target_pairs={{12,0},{16,4},{20,8},{24,12},{28,16},{32,20},{36,24},{40,28},{44,3... | collective-permute-start | bytes 7688 | tf_op jit(solution)/shard_map/ppermute | solution.py:14
  97.3 7.6 %collective-permute-start.19 = (bf16[4,320]{1,0:T(4,128)(2,1)S(1)}, bf16[4,320]{1,0:T(4,128)(2,1)S(1)}, u32[]{:S(2)}, u32[]{:S(2)}) collective-permute-start(bf16[4,320]{1,0:T(4,128)(2,1)S(1)} %get-tuple-element.34), channel_id=1, source_target_pairs={{16,0},{20,4},{24,8},{28,12},{32,16},{36,20},{40,24},{44,28},{48,3... | collective-permute-start | bytes 7688 | tf_op jit(solution)/shard_map/ppermute | solution.py:14
  104.9 9.2 %collective-permute-start.20 = (bf16[4,320]{1,0:T(4,128)(2,1)S(1)}, bf16[4,320]{1,0:T(4,128)(2,1)S(1)}, u32[]{:S(2)}, u32[]{:S(2)}) collective-permute-start(bf16[4,320]{1,0:T(4,128)(2,1)S(1)} %get-tuple-element.33), channel_id=1, source_target_pairs={{508,0},{0,4},{4,8},{8,12},{12,16},{16,20},{20,24},{24,28},{28,32}... | collective-permute-start | bytes 7688 | tf_op jit(solution)/shard_map/ppermute | solution.py:14
  125.9 15.7 %collective-permute-start.23 = (bf16[4,320]{1,0:T(4,128)(2,1)S(1)}, bf16[4,320]{1,0:T(4,128)(2,1)S(1)}, u32[]{:S(2)}, u32[]{:S(2)}) collective-permute-start(bf16[4,320]{1,0:T(4,128)(2,1)S(1)} %get-tuple-element.30), channel_id=1, source_target_pairs={{496,0},{500,4},{504,8},{508,12},{0,16},{4,20},{8,24},{12,28},{16,... | collective-permute-start | bytes 7688 | tf_op jit(solution)/shard_map/ppermute | solution.py:14
  141.6 15.6 %collective-permute-start.12 = (f32[4,320]{1,0:T(4,128)S(1)}, f32[4,320]{1,0:T(4,128)S(1)}, u32[]{:S(2)}, u32[]{:S(2)}) collective-permute-start(f32[4,320]{1,0:T(4,128)S(1)} %get-tuple-element.17), channel_id=1, source_target_pairs={{4,0},{8,4},{12,8},{16,12},{20,16},{24,20},{28,24},{32,28},{36,32}... | collective-permute-start | bytes 15368 | tf_op jit(solution)/shard_map/ppermute | solution.py:14
  145.1 12.2 %collective-permute-start.13 = (f32[4,320]{1,0:T(4,128)S(1)}, f32[4,320]{1,0:T(4,128)S(1)}, u32[]{:S(2)}, u32[]{:S(2)}) collective-permute-start(f32[4,320]{1,0:T(4,128)S(1)} %get-tuple-element.16), channel_id=1, source_target_pairs={{8,0},{12,4},{16,8},{20,12},{24,16},{28,20},{32,24},{36,28},{40,32... | collective-permute-start | bytes 15368 | tf_op jit(solution)/shard_map/ppermute | solution.py:14
  148.5 8.8 %collective-permute-start.14 = (f32[4,320]{1,0:T(4,128)S(1)}, f32[4,320]{1,0:T(4,128)S(1)}, u32[]{:S(2)}, u32[]{:S(2)}) collective-permute-start(f32[4,320]{1,0:T(4,128)S(1)} %get-tuple-element.15), channel_id=1, source_target_pairs={{12,0},{16,4},{20,8},{24,12},{28,16},{32,20},{36,24},{40,28},{44,3... | collective-permute-start | bytes 15368 | tf_op jit(solution)/shard_map/ppermute | solution.py:14
  155.3 7.6 %collective-permute-start.15 = (f32[4,320]{1,0:T(4,128)S(1)}, f32[4,320]{1,0:T(4,128)S(1)}, u32[]{:S(2)}, u32[]{:S(2)}) collective-permute-start(f32[4,320]{1,0:T(4,128)S(1)} %get-tuple-element.14), channel_id=1, source_target_pairs={{16,0},{20,4},{24,8},{28,12},{32,16},{36,20},{40,24},{44,28},{48,3... | collective-permute-start | bytes 15368 | tf_op jit(solution)/shard_map/ppermute | solution.py:14
  194.1 13.3 %collective-permute-start.32 = (bf16[4,320]{1,0:T(4,128)(2,1)S(1)}, bf16[4,320]{1,0:T(4,128)(2,1)S(1)}, u32[]{:S(2)}, u32[]{:S(2)}) collective-permute-start(bf16[4,320]{1,0:T(4,128)(2,1)S(1)} %get-tuple-element.29), channel_id=1, source_target_pairs={{4,0},{8,4},{12,8},{16,12},{20,16},{24,20},{28,24},{32,28},{36,32}... | collective-permute-start | bytes 7688 | tf_op jit(solution)/shard_map/ppermute | solution.py:14
  197.5 70.4 %collective-permute-start.24 = (f32[4,320]{1,0:T(4,128)S(1)}, f32[4,320]{1,0:T(4,128)S(1)}, u32[]{:S(2)}, u32[]{:S(2)}) collective-permute-start(f32[4,320]{1,0:T(4,128)S(1)} %get-tuple-element.13), channel_id=1, source_target_pairs={{508,0},{0,4},{4,8},{8,12},{12,16},{16,20},{20,24},{24,28},{28,32}... | collective-permute-start | bytes 15368 | tf_op jit(solution)/shard_map/ppermute | solution.py:14
  199.9 71.4 %collective-permute-start.25 = (f32[4,320]{1,0:T(4,128)S(1)}, f32[4,320]{1,0:T(4,128)S(1)}, u32[]{:S(2)}, u32[]{:S(2)}) collective-permute-start(f32[4,320]{1,0:T(4,128)S(1)} %get-tuple-element.12), channel_id=1, source_target_pairs={{504,0},{508,4},{0,8},{4,12},{8,16},{12,20},{16,24},{20,28},{24,32... | collective-permute-start | bytes 15368 | tf_op jit(solution)/shard_map/ppermute | solution.py:14
  203.6 74.6 %collective-permute-start.26 = (f32[4,320]{1,0:T(4,128)S(1)}, f32[4,320]{1,0:T(4,128)S(1)}, u32[]{:S(2)}, u32[]{:S(2)}) collective-permute-start(f32[4,320]{1,0:T(4,128)S(1)} %get-tuple-element.11), channel_id=1, source_target_pairs={{500,0},{504,4},{508,8},{0,12},{4,16},{8,20},{12,24},{16,28},{20,3... | collective-permute-start | bytes 15368 | tf_op jit(solution)/shard_map/ppermute | solution.py:14
  205.5 74.6 %collective-permute-start.27 = (f32[4,320]{1,0:T(4,128)S(1)}, f32[4,320]{1,0:T(4,128)S(1)}, u32[]{:S(2)}, u32[]{:S(2)}) collective-permute-start(f32[4,320]{1,0:T(4,128)S(1)} %get-tuple-element.10), channel_id=1, source_target_pairs={{496,0},{500,4},{504,8},{508,12},{0,16},{4,20},{8,24},{12,28},{16,... | collective-permute-start | bytes 15368 | tf_op jit(solution)/shard_map/ppermute | solution.py:14
  220.1 7.6 %collective-permute-start.35 = (bf16[4,320]{1,0:T(4,128)(2,1)S(1)}, bf16[4,320]{1,0:T(4,128)(2,1)S(1)}, u32[]{:S(2)}, u32[]{:S(2)}) collective-permute-start(bf16[4,320]{1,0:T(4,128)(2,1)S(1)} %get-tuple-element.26), channel_id=1, source_target_pairs={{16,0},{20,4},{24,8},{28,12},{32,16},{36,20},{40,24},{44,28},{48,3... | collective-permute-start | bytes 7688 | tf_op jit(solution)/shard_map/ppermute | solution.py:14
  227.7 9.2 %collective-permute-start.36 = (bf16[4,320]{1,0:T(4,128)(2,1)S(1)}, bf16[4,320]{1,0:T(4,128)(2,1)S(1)}, u32[]{:S(2)}, u32[]{:S(2)}) collective-permute-start(bf16[4,320]{1,0:T(4,128)(2,1)S(1)} %get-tuple-element.25), channel_id=1, source_target_pairs={{508,0},{0,4},{4,8},{8,12},{12,16},{16,20},{20,24},{24,28},{28,32}... | collective-permute-start | bytes 7688 | tf_op jit(solution)/shard_map/ppermute | solution.py:14
  250.2 14.3 %collective-permute-start.39 = (bf16[4,320]{1,0:T(4,128)(2,1)S(1)}, bf16[4,320]{1,0:T(4,128)(2,1)S(1)}, u32[]{:S(2)}, u32[]{:S(2)}) collective-permute-start(bf16[4,320]{1,0:T(4,128)(2,1)S(1)} %get-tuple-element.22), channel_id=1, source_target_pairs={{496,0},{500,4},{504,8},{508,12},{0,16},{4,20},{8,24},{12,28},{16,... | collective-permute-start | bytes 7688 | tf_op jit(solution)/shard_map/ppermute | solution.py:14
  264.5 15.6 %collective-permute-start.28 = (f32[4,320]{1,0:T(4,128)S(1)}, f32[4,320]{1,0:T(4,128)S(1)}, u32[]{:S(2)}, u32[]{:S(2)}) collective-permute-start(f32[4,320]{1,0:T(4,128)S(1)} %get-tuple-element.9), channel_id=1, source_target_pairs={{4,0},{8,4},{12,8},{16,12},{20,16},{24,20},{28,24},{32,28},{36,32}... | collective-permute-start | bytes 15368 | tf_op jit(solution)/shard_map/ppermute | solution.py:14
  267.9 12.2 %collective-permute-start.29 = (f32[4,320]{1,0:T(4,128)S(1)}, f32[4,320]{1,0:T(4,128)S(1)}, u32[]{:S(2)}, u32[]{:S(2)}) collective-permute-start(f32[4,320]{1,0:T(4,128)S(1)} %get-tuple-element.8), channel_id=1, source_target_pairs={{8,0},{12,4},{16,8},{20,12},{24,16},{28,20},{32,24},{36,28},{40,32... | collective-permute-start | bytes 15368 | tf_op jit(solution)/shard_map/ppermute | solution.py:14
  271.3 8.8 %collective-permute-start.30 = (f32[4,320]{1,0:T(4,128)S(1)}, f32[4,320]{1,0:T(4,128)S(1)}, u32[]{:S(2)}, u32[]{:S(2)}) collective-permute-start(f32[4,320]{1,0:T(4,128)S(1)} %get-tuple-element.7), channel_id=1, source_target_pairs={{12,0},{16,4},{20,8},{24,12},{28,16},{32,20},{36,24},{40,28},{44,3... | collective-permute-start | bytes 15368 | tf_op jit(solution)/shard_map/ppermute | solution.py:14
  278.1 7.6 %collective-permute-start.31 = (f32[4,320]{1,0:T(4,128)S(1)}, f32[4,320]{1,0:T(4,128)S(1)}, u32[]{:S(2)}, u32[]{:S(2)}) collective-permute-start(f32[4,320]{1,0:T(4,128)S(1)} %get-tuple-element.6), channel_id=1, source_target_pairs={{16,0},{20,4},{24,8},{28,12},{32,16},{36,20},{40,24},{44,28},{48,3... | collective-permute-start | bytes 15368 | tf_op jit(solution)/shard_map/ppermute | solution.py:14
  (12 other events, 271.6 us)
